TPU v7x, 32 devices: a whole 2x2x4 slice. The times are simulated.
32 devices in a mesh: slab: 4 (over y, x), cross: 8 (over z, core).
Axes of the slice: x: 2, y: 2, z: 4, core: 2. Of those that a mesh axis runs over, the one named last changes fastest.
Arguments:
- rhs: bfloat16 [4, 8, 32, 128, 128], P('slab', 'cross'), may hold values from -6 to 6
- m_blocks: bfloat16 [4, 8, 56, 3, 128, 128], P('slab', 'cross'), may hold values from -0.3125 to 0.3125
- m_cols: int32 [4, 8, 56, 3], P('slab', 'cross'), may hold values from 0 to 55, as said below
- j_blocks: bfloat16 [4, 8, 32, 3, 128, 128], P('slab', 'cross'), may hold values from -0.3125 to 0.3125
- j_cols: int32 [4, 8, 32, 3], P('slab', 'cross'), may hold values from 0 to 55, as said below
- send_list: int32 [4, 8, 8, 2], P('slab', 'cross'), may hold values from 0 to 31, as said below
- send_count: int32 [4, 8, 8], P('slab', 'cross'), may hold values from 0 to 2, as said below
Outputs:
- second_iterate: bfloat16 [4, 8, 32, 128, 128], P('slab', 'cross')
Inputs may be any that keep to these rules, and one draw needn't show every extreme that they name: `m_cols`: each row's first block column is the row itself; the others differ from it and from each other. `j_cols`: each row's first block column is the row itself; the others differ from it and from each other. `send_list`: the used slots of one list name different block rows. `send_count`: no subdomain lends rows to itself; in every slab index some subdomain receives 2 rows from each other one.
All inputs are finite; a program needn't handle non-finite values.
Results may differ from a plain program's by a relative error of at most 0.0058.
Values may be sent and summed in bfloat16 or wider, within the bound.
A program may use at most 64 MiB of HBM per device.

v0:
```python
import jax
import jax.numpy as jnp
from jax import lax
from jax.sharding import PartitionSpec as P

OVL = 4


def extended_2(cells, sides, width):
    for axis, dim in sides:
        count = lax.axis_size(axis)
        ends = count - 1
        head = lax.slice_in_dim(cells, 0, width, axis=dim)
        tail = lax.slice_in_dim(cells, cells.shape[dim] - width, cells.shape[dim], axis=dim)
        cells = jnp.concatenate(
            [
                lax.ppermute(tail, axis, [(i, (i + 1) % count) for i in range(ends)]),
                cells,
                lax.ppermute(head, axis, [((i + 1) % count, i) for i in range(ends)]),
            ],
            axis=dim,
        )
    return cells


def route(buffer):
    return lax.all_to_all(buffer, "cross", split_axis=0, concat_axis=0, tiled=True)


def per_device(rhs, m_blocks, m_cols, j_blocks, j_cols, send_list, send_count):
    rhs_own = rhs[0, 0]
    inverse = m_blocks[0, 0]
    inverse_cols = m_cols[0, 0]
    jacobian = j_blocks[0, 0]
    jacobian_cols = j_cols[0, 0]
    targets = send_list[0, 0]
    counts = send_count[0, 0]
    owned = rhs_own.shape[0]
    block_size = rhs_own.shape[1]
    vectors = rhs_own.shape[2]
    peer_count = targets.shape[0]
    slot_count = targets.shape[1]
    valid = jnp.arange(slot_count, dtype=jnp.int32)[None, :] < counts[:, None]
    flat_targets = targets.reshape(-1)
    flat_valid = valid.reshape(-1)
    scatter_table = (
        (flat_targets[None, :] == jnp.arange(owned, dtype=jnp.int32)[:, None]) & flat_valid[None, :]
    ).astype(jnp.bfloat16)

    def extend(field):
        padded = extended_2(field, (("slab", 0),), OVL)
        outgoing = jnp.take(field, flat_targets, axis=0)
        outgoing = jnp.where(flat_valid[:, None, None], outgoing, jnp.zeros((), jnp.bfloat16))
        incoming = route(outgoing.reshape(peer_count, slot_count, block_size, vectors))
        return jnp.concatenate(
            [field, padded[:OVL], padded[owned + OVL :], incoming.reshape(-1, block_size, vectors)],
            axis=0,
        )

    def apply_set(blocks, columns, extended):
        picked = jnp.take(extended, columns, axis=0)
        return lax.dot_general(
            blocks, picked, (((1, 3), (1, 2)), ((0,), (0,))), preferred_element_type=jnp.float32
        )

    def precondition(field):
        extended = extend(field)
        partial_value = apply_set(inverse, inverse_cols, extended).astype(jnp.bfloat16)
        returned_slab = extended_2(partial_value[owned : owned + 2 * OVL], (("slab", 0),), OVL)
        cross_part = partial_value[owned + 2 * OVL :].reshape(
            peer_count, slot_count, block_size, vectors
        )
        returned_cross = route(cross_part).reshape(peer_count * slot_count, block_size * vectors)
        total = partial_value[:owned].astype(jnp.float32)
        total = total.at[:OVL].add(returned_slab[:OVL].astype(jnp.float32))
        total = total.at[owned - OVL :].add(returned_slab[3 * OVL :].astype(jnp.float32))
        added = jnp.dot(scatter_table, returned_cross, preferred_element_type=jnp.float32)
        return total + added.reshape(owned, block_size, vectors)

    first = precondition(rhs_own).astype(jnp.bfloat16)
    image = apply_set(jacobian, jacobian_cols, extend(first))
    residual = (rhs_own.astype(jnp.float32) - image).astype(jnp.bfloat16)
    second = (first.astype(jnp.float32) + precondition(residual)).astype(jnp.bfloat16)
    return second[None, None]


def solution(mesh):
    return jax.shard_map(
        per_device,
        mesh=mesh,
        in_specs=(
            P("slab", "cross", None, None, None),
            P("slab", "cross", None, None, None, None),
            P("slab", "cross", None, None),
            P("slab", "cross", None, None, None, None),
            P("slab", "cross", None, None),
            P("slab", "cross", None, None),
            P("slab", "cross", None),
        ),
        out_specs=P("slab", "cross", None, None, None),
        check_vma=False,
    )
```

profile of v0, /device:TPU:0, one launch (start us, length us, event | category | flops | bytes accessed | tf_op | source)
XLA Modules:
  0.0 200.1 jit_solution(8047308100709695920)
XLA Ops:
  1.0 2.3 %copy.20 = bf16[1,1,32,128,128]{3,4,2,1,0:T(8,128)(2,1)} copy(bf16[1,1,32,128,128]{4,3,2,1,0:T(8,128)(2,1)} %param.19) | data formatting | bytes 2097152 | tf_op args[0]
  3.5 2.7 %gather_fusion.1 = bf16[16,128,128]{1,2,0:T(8,128)(2,1)} fusion(bf16[32,128,128]{1,2,0:T(8,128)(2,1)} %bitcast.101, s32[1024]{0:T(1024)S(1)} %pad_clamp_fusion.2), kind=kCustom, calls=%fused_computation.clone | custom fusion | bytes 1048640 | tf_op jit(solution)/shard_map/jit(_take)/gather | solution.py:52
  6.1 2.0 select_select_fusion.2
  8.1 6.4 %all-to-all-start = ((bf16[8,2,128,128]{2,3,1,0:T(8,128)(2,1)}), bf16[8,2,128,128]{2,3,1,0:T(8,128)(2,1)}, u32[]{:S(2)}, u32[]{:S(2)}) async-start(bf16[8,2,128,128]{2,3,1,0:T(8,128)(2,1)} %bitcast.106), calls=%async_computation | async-start | bytes 1048576 | tf_op jit(solution)/shard_map/all_to_all | solution.py:27
  16.1 3.4 %collective-permute-start = (bf16[4,128,128]{1,2,0:T(8,128)(2,1)}, bf16[4,128,128]{1,2,0:T(8,128)(2,1)S(1)}, u32[]{:S(2)}, u32[]{:S(2)}) collective-permute-start(bf16[4,128,128]{1,2,0:T(8,128)(2,1)} %get-tuple-element.63), channel_id=1, source_target_pairs={{0,8},{8,16},{16,24},{1,9},{9,17},{17,25},{2,10},{10,18},{18,26},{... | collective-permute-start | bytes 393224 | tf_op jit(solution)/shard_map/ppermute | solution.py:17
  24.4 3.5 %collective-permute-done.1 = bf16[4,128,128]{1,2,0:T(8,128)(2,1)S(1)} collective-permute-done((bf16[4,128,128]{1,2,0:T(8,128)(2,1)S(1)}, bf16[4,128,128]{1,2,0:T(8,128)(2,1)S(1)}, u32[]{:S(2)}, u32[]{:S(2)}) %collective-permute-start.1) | collective-permute-done | bytes 131104 | tf_op jit(solution)/shard_map/ppermute | solution.py:19
  27.9 2.0 %all-to-all-done = bf16[8,2,128,128]{2,3,1,0:T(8,128)(2,1)} async-done(((bf16[8,2,128,128]{2,3,1,0:T(8,128)(2,1)}), bf16[8,2,128,128]{2,3,1,0:T(8,128)(2,1)}, u32[]{:S(2)}, u32[]{:S(2)}) %all-to-all-start) | async-done | bytes 524320 | tf_op jit(solution)/shard_map/all_to_all | solution.py:27
  29.9 2.9 %pad_maximum_fusion = bf16[56,128,128]{1,2,0:T(8,128)(2,1)} fusion(bf16[16,128,128]{1,2,0:T(8,128)(2,1)} %bitcast.5, bf16[4,128,128]{1,2,0:T(8,128)(2,1)S(1)} %collective-permute-done.1, bf16[4,128,128]{1,2,0:T(8,128)(2,1)S(1)} %collective-permute-done, bf16[32,128,128]{1,2,0:T(8,128)(2,1)} %bitcast.102), kind=kLoop, calls=%fused_computation.28 | loop fusion | flops 2752512 | bytes 3670016 | tf_op jit(solution)/shard_map/concatenate | solution.py:55
  32.8 9.3 %gather_fusion.2 = bf16[168,128,128]{1,2,0:T(8,128)(2,1)} fusion(bf16[56,128,128]{1,2,0:T(8,128)(2,1)} %pad_maximum_fusion, s32[1024]{0:T(1024)S(1)} %pad_clamp_fusion.1), kind=kCustom, calls=%fused_computation.1.clone | custom fusion | bytes 11010720 | tf_op jit(solution)/shard_map/jit(_take)/gather | solution.py:61
  42.1 6.6 %fusion.15 = bf16[56,128,128]{1,2,0:T(8,128)(2,1)S(1)} fusion(bf16[1,1,56,3,128,128]{5,4,3,2,1,0:T(8,128)(2,1)} %param.20, bf16[56,3,128,128]{2,3,1,0:T(8,128)(2,1)} %bitcast.104, pred[56,3]{1,0:T(8,128)(4,1)S(1)} %copy-done.3), kind=kOutput, calls=%fused_computation.26 | convolution fusion | flops 708313088 | bytes 12845224 | tf_op jit(solution)/shard_map/dot_general | solution.py:62
  50.8 2.0 %copy.25 = bf16[8,2,128,128]{3,2,1,0:T(8,128)(2,1)} copy(bf16[8,2,128,128]{2,3,1,0:T(8,128)(2,1)} %bitcast.109) | data formatting | bytes 1048576 | tf_op jit(solution)/shard_map/reshape | solution.py:70
  52.9 4.1 %all-to-all-start.1 = ((bf16[8,2,128,128]{3,2,1,0:T(8,128)(2,1)}), bf16[8,2,128,128]{3,2,1,0:T(8,128)(2,1)}, u32[]{:S(2)}, u32[]{:S(2)}) async-start(bf16[8,2,128,128]{3,2,1,0:T(8,128)(2,1)} %copy.25), calls=%async_computation.1 | async-start | bytes 1048576 | tf_op jit(solution)/shard_map/all_to_all | solution.py:27
  58.0 3.4 %collective-permute-start.2 = (bf16[4,128,128]{1,2,0:T(8,128)(2,1)S(1)}, bf16[4,128,128]{1,2,0:T(8,128)(2,1)S(1)}, u32[]{:S(2)}, u32[]{:S(2)}) collective-permute-start(bf16[4,128,128]{1,2,0:T(8,128)(2,1)S(1)} %get-tuple-element.58), channel_id=1, source_target_pairs={{0,8},{8,16},{16,24},{1,9},{9,17},{17,25},{2,10},{10,18},{18,26},{... | collective-permute-start | bytes 393224 | tf_op jit(solution)/shard_map/ppermute | solution.py:17
  61.4 2.8 %slice_convert_fusion.1 = f32[32,128,128]{1,2,0:T(8,128)} fusion(bf16[56,128,128]{1,2,0:T(8,128)(2,1)} %copy-done.2), kind=kLoop, calls=%fused_computation.34 | loop fusion | flops 524288 | bytes 3145728 | tf_op jit(solution)/shard_map/convert_element_type | solution.py:74
  65.5 1.7 fusion.40
  67.2 4.4 %collective-permute-done.3 = bf16[4,128,128]{1,2,0:T(8,128)(2,1)S(1)} collective-permute-done((bf16[4,128,128]{1,2,0:T(8,128)(2,1)S(1)}, bf16[4,128,128]{1,2,0:T(8,128)(2,1)S(1)}, u32[]{:S(2)}, u32[]{:S(2)}) %collective-permute-start.3) | collective-permute-done | bytes 131104 | tf_op jit(solution)/shard_map/ppermute | solution.py:19
  71.6 1.7 fusion.39
  73.3 3.0 %fusion.34 = f32[32,128,128]{2,0,1:T(8,128)} fusion(s32[16]{0:T(128)S(1)} %copy-done.11, pred[16]{0:T(512)(128)(4,1)S(1)} %lt.60, bf16[2,8,128,128]{3,2,1,0:T(8,128)(2,1)} %bitcast.40), kind=kOutput, calls=%fused_computation.40 | convolution fusion | flops 16778240 | bytes 2621520 | tf_op jit(solution)/shard_map/dot_general | solution.py:77
  76.3 3.0 %copy.27 = f32[32,128,128]{1,2,0:T(8,128)} copy(f32[32,128,128]{2,0,1:T(8,128)} %fusion.34) | data formatting | bytes 4194304 | tf_op jit(solution)/shard_map/dot_general | solution.py:77
  79.3 3.6 %add_convert_fusion.1 = bf16[32,128,128]{1,2,0:T(8,128)(2,1)} fusion(f32[32,128,128]{1,2,0:T(8,128)} %fusion.39, f32[32,128,128]{1,2,0:T(8,128)} %copy.27), kind=kLoop, calls=%fused_computation.25 | loop fusion | flops 1048576 | bytes 5242880 | tf_op jit(solution)/shard_map/convert_element_type | solution.py:80
  82.9 2.7 %gather_fusion.3 = bf16[16,128,128]{1,2,0:T(8,128)(2,1)} fusion(bf16[32,128,128]{1,2,0:T(8,128)(2,1)} %add_convert_fusion.1, s32[1024]{0:T(1024)S(1)} %pad_clamp_fusion.2), kind=kCustom, calls=%fused_computation.2.clone | custom fusion | bytes 1048640 | tf_op jit(solution)/shard_map/jit(_take)/gather | solution.py:52
  85.6 2.0 %select_select_fusion.1 = bf16[16,128,128]{1,2,0:T(8,128)(2,1)} fusion(bf16[16,128,128]{1,2,0:T(8,128)(2,1)} %gather_fusion.3, pred[16]{0:T(512)(128)(4,1)S(1)} %copy-done.8, pred[16]{0:T(512)(128)(4,1)S(1)} %lt.60), kind=kLoop, calls=%fused_computation.44 | loop fusion | flops 524288 | bytes 1048608 | tf_op jit(solution)/shard_map/jit(_where)/select_n | solution.py:53
  87.6 4.7 %all-to-all-start.2 = ((bf16[8,2,128,128]{2,3,1,0:T(8,128)(2,1)}), bf16[8,2,128,128]{2,3,1,0:T(8,128)(2,1)}, u32[]{:S(2)}, u32[]{:S(2)}) async-start(bf16[8,2,128,128]{2,3,1,0:T(8,128)(2,1)} %bitcast.107), calls=%async_computation.2 | async-start | bytes 1048576 | tf_op jit(solution)/shard_map/all_to_all | solution.py:27
  94.6 4.3 %collective-permute-start.4 = (bf16[4,128,128]{1,2,0:T(8,128)(2,1)}, bf16[4,128,128]{1,2,0:T(8,128)(2,1)S(1)}, u32[]{:S(2)}, u32[]{:S(2)}) collective-permute-start(bf16[4,128,128]{1,2,0:T(8,128)(2,1)} %get-tuple-element.61), channel_id=1, source_target_pairs={{0,8},{8,16},{16,24},{1,9},{9,17},{17,25},{2,10},{10,18},{18,26},{... | collective-permute-start | bytes 393224 | tf_op jit(solution)/shard_map/ppermute | solution.py:17
  107.8 2.9 %pad_maximum_fusion.1 = bf16[56,128,128]{1,2,0:T(8,128)(2,1)} fusion(bf16[16,128,128]{1,2,0:T(8,128)(2,1)} %bitcast.15, bf16[4,128,128]{1,2,0:T(8,128)(2,1)S(1)} %collective-permute-done.5, bf16[4,128,128]{1,2,0:T(8,128)(2,1)S(1)} %collective-permute-done.4, bf16[32,128,128]{1,2,0:T(8,128)(2,1)} %add_convert_fusion.1), kind=kLoop, calls=%fused_computation.29 | loop fusion | flops 2752512 | bytes 3670016 | tf_op jit(solution)/shard_map/concatenate | solution.py:55
  110.7 4.2 %gather_fusion = bf16[96,128,128]{1,2,0:T(8,128)(2,1)} fusion(bf16[56,128,128]{1,2,0:T(8,128)(2,1)} %pad_maximum_fusion.1, s32[1024]{0:T(1024)S(1)} %pad_clamp_fusion), kind=kCustom, calls=%fused_computation.5 | custom fusion | bytes 6291840 | tf_op jit(solution)/shard_map/jit(_take)/gather | solution.py:61
  114.8 4.6 %fusion.14 = bf16[32,128,128]{1,2,0:T(8,128)(2,1)} fusion(bf16[1,1,32,3,128,128]{5,4,3,2,1,0:T(8,128)(2,1)S(1)} %copy-done, bf16[32,3,128,128]{2,3,1,0:T(8,128)(2,1)} %bitcast.105, pred[32,3]{1,0:T(8,128)(4,1)S(1)} %copy-done.13, bf16[1,1,32,128,128]{3,4,2,1,0:T(8,128)(2,1)} %copy.20), kind=kOutput, calls=%fused_computation.23 | convolution fusion | flops 405798912 | bytes 8388704 | tf_op jit(solution)/shard_map/dot_general | solution.py:62
  119.5 2.6 %gather_fusion.4 = bf16[16,128,128]{1,2,0:T(8,128)(2,1)} fusion(bf16[32,128,128]{1,2,0:T(8,128)(2,1)} %fusion.14, s32[1024]{0:T(1024)S(1)} %pad_clamp_fusion.2), kind=kCustom, calls=%fused_computation.3.clone | custom fusion | bytes 1048640 | tf_op jit(solution)/shard_map/jit(_take)/gather | solution.py:52
  122.1 2.0 select_select_fusion
  124.1 4.1 %all-to-all-start.3 = ((bf16[8,2,128,128]{2,3,1,0:T(8,128)(2,1)}), bf16[8,2,128,128]{2,3,1,0:T(8,128)(2,1)}, u32[]{:S(2)}, u32[]{:S(2)}) async-start(bf16[8,2,128,128]{2,3,1,0:T(8,128)(2,1)} %bitcast.108), calls=%async_computation.3 | async-start | bytes 1048576 | tf_op jit(solution)/shard_map/all_to_all | solution.py:27
  129.2 4.3 %collective-permute-start.6 = (bf16[4,128,128]{1,2,0:T(8,128)(2,1)S(1)}, bf16[4,128,128]{1,2,0:T(8,128)(2,1)S(1)}, u32[]{:S(2)}, u32[]{:S(2)}) collective-permute-start(bf16[4,128,128]{1,2,0:T(8,128)(2,1)S(1)} %get-tuple-element.59), channel_id=1, source_target_pairs={{0,8},{8,16},{16,24},{1,9},{9,17},{17,25},{2,10},{10,18},{18,26},{... | collective-permute-start | bytes 393224 | tf_op jit(solution)/shard_map/ppermute | solution.py:17
  135.0 1.8 collective-permute-done.6
  136.8 4.1 %collective-permute-done.7 = bf16[4,128,128]{1,2,0:T(8,128)(2,1)S(1)} collective-permute-done((bf16[4,128,128]{1,2,0:T(8,128)(2,1)S(1)}, bf16[4,128,128]{1,2,0:T(8,128)(2,1)S(1)}, u32[]{:S(2)}, u32[]{:S(2)}) %collective-permute-start.7) | collective-permute-done | bytes 131104 | tf_op jit(solution)/shard_map/ppermute | solution.py:19
  140.9 2.6 %all-to-all-done.3 = bf16[8,2,128,128]{2,3,1,0:T(8,128)(2,1)} async-done(((bf16[8,2,128,128]{2,3,1,0:T(8,128)(2,1)}), bf16[8,2,128,128]{2,3,1,0:T(8,128)(2,1)}, u32[]{:S(2)}, u32[]{:S(2)}) %all-to-all-start.3) | async-done | bytes 524320 | tf_op jit(solution)/shard_map/all_to_all | solution.py:27
  143.6 2.9 %pad_maximum_fusion.2 = bf16[56,128,128]{1,2,0:T(8,128)(2,1)} fusion(bf16[16,128,128]{1,2,0:T(8,128)(2,1)} %bitcast.23, bf16[4,128,128]{1,2,0:T(8,128)(2,1)S(1)} %collective-permute-done.7, bf16[4,128,128]{1,2,0:T(8,128)(2,1)S(1)} %collective-permute-done.6, bf16[32,128,128]{1,2,0:T(8,128)(2,1)} %fusion.14), kind=kLoop, calls=%fused_computation.30 | loop fusion | flops 2752512 | bytes 3670016 | tf_op jit(solution)/shard_map/concatenate | solution.py:55
  146.4 9.3 %gather_fusion.5 = bf16[168,128,128]{1,2,0:T(8,128)(2,1)} fusion(bf16[56,128,128]{1,2,0:T(8,128)(2,1)} %pad_maximum_fusion.2, s32[1024]{0:T(1024)S(1)} %pad_clamp_fusion.1), kind=kCustom, calls=%fused_computation.4.clone | custom fusion | bytes 11010720 | tf_op jit(solution)/shard_map/jit(_take)/gather | solution.py:61
  155.8 6.6 %fusion.16 = bf16[56,128,128]{1,2,0:T(8,128)(2,1)S(1)} fusion(bf16[1,1,56,3,128,128]{5,4,3,2,1,0:T(8,128)(2,1)} %param.20, bf16[56,3,128,128]{2,3,1,0:T(8,128)(2,1)} %bitcast.103, pred[56,3]{1,0:T(8,128)(4,1)S(1)} %copy-done.4), kind=kOutput, calls=%fused_computation.27 | convolution fusion | flops 708313088 | bytes 12845224 | tf_op jit(solution)/shard_map/dot_general | solution.py:62
  164.5 2.0 %copy.32 = bf16[8,2,128,128]{3,2,1,0:T(8,128)(2,1)} copy(bf16[8,2,128,128]{2,3,1,0:T(8,128)(2,1)} %bitcast.110) | data formatting | bytes 1048576 | tf_op jit(solution)/shard_map/reshape | solution.py:70
  166.5 4.1 %all-to-all-start.4 = ((bf16[8,2,128,128]{3,2,1,0:T(8,128)(2,1)}), bf16[8,2,128,128]{3,2,1,0:T(8,128)(2,1)}, u32[]{:S(2)}, u32[]{:S(2)}) async-start(bf16[8,2,128,128]{3,2,1,0:T(8,128)(2,1)} %copy.32), calls=%async_computation.4 | async-start | bytes 1048576 | tf_op jit(solution)/shard_map/all_to_all | solution.py:27
  171.6 4.3 %collective-permute-start.8 = (bf16[4,128,128]{1,2,0:T(8,128)(2,1)S(1)}, bf16[4,128,128]{1,2,0:T(8,128)(2,1)S(1)}, u32[]{:S(2)}, u32[]{:S(2)}) collective-permute-start(bf16[4,128,128]{1,2,0:T(8,128)(2,1)S(1)} %get-tuple-element.56), channel_id=1, source_target_pairs={{0,8},{8,16},{16,24},{1,9},{9,17},{17,25},{2,10},{10,18},{18,26},{... | collective-permute-start | bytes 393224 | tf_op jit(solution)/shard_map/ppermute | solution.py:17
  176.0 2.8 %slice_convert_fusion = f32[32,128,128]{1,2,0:T(8,128)} fusion(bf16[56,128,128]{1,2,0:T(8,128)(2,1)} %copy-done.1), kind=kLoop, calls=%fused_computation.33 | loop fusion | flops 524288 | bytes 3145728 | tf_op jit(solution)/shard_map/convert_element_type | solution.py:74
  180.1 1.7 fusion.38
  181.7 4.4 %collective-permute-done.9 = bf16[4,128,128]{1,2,0:T(8,128)(2,1)S(1)} collective-permute-done((bf16[4,128,128]{1,2,0:T(8,128)(2,1)S(1)}, bf16[4,128,128]{1,2,0:T(8,128)(2,1)S(1)}, u32[]{:S(2)}, u32[]{:S(2)}) %collective-permute-start.9) | collective-permute-done | bytes 131104 | tf_op jit(solution)/shard_map/ppermute | solution.py:19
  186.1 1.7 fusion.37
  187.8 3.0 %fusion.31 = f32[32,128,128]{2,0,1:T(8,128)} fusion(s32[16]{0:T(128)S(1)} %copy-done.12, pred[16]{0:T(512)(128)(4,1)S(1)} %lt.60, bf16[2,8,128,128]{3,2,1,0:T(8,128)(2,1)} %bitcast.44), kind=kOutput, calls=%fused_computation.37 | convolution fusion | flops 16778240 | bytes 2621520 | tf_op jit(solution)/shard_map/dot_general | solution.py:77
  190.8 3.0 %copy.34 = f32[32,128,128]{1,2,0:T(8,128)} copy(f32[32,128,128]{2,0,1:T(8,128)} %fusion.31) | data formatting | bytes 4194304 | tf_op jit(solution)/shard_map/dot_general | solution.py:77
  193.8 4.1 %fusion.30 = bf16[1,1,32,128,128]{3,4,2,1,0:T(8,128)(2,1)} fusion(f32[32,128,128]{1,2,0:T(8,128)} %fusion.37, f32[32,128,128]{1,2,0:T(8,128)} %copy.34, bf16[32,128,128]{1,2,0:T(8,128)(2,1)} %add_convert_fusion.1), kind=kLoop, calls=%fused_computation.32 | loop fusion | flops 2097152 | bytes 6291456 | tf_op jit(solution)/shard_map/broadcast_in_dim | solution.py:84
  197.9 2.3 %copy.35 = bf16[1,1,32,128,128]{4,3,2,1,0:T(8,128)(2,1)} copy(bf16[1,1,32,128,128]{3,4,2,1,0:T(8,128)(2,1)} %fusion.30) | data formatting | bytes 2097152 | tf_op jit(solution)/shard_map/broadcast_in_dim | solution.py:84
  (69 shorter events, 30.0 us)
Async XLA Ops:
  0.0 114.8 %copy-start = (bf16[1,1,32,3,128,128]{5,4,3,2,1,0:T(8,128)(2,1)S(1)}, bf16[1,1,32,3,128,128]{5,4,3,2,1,0:T(8,128)(2,1)}, u32[]{:S(2)}) copy-start(bf16[1,1,32,3,128,128]{5,4,3,2,1,0:T(8,128)(2,1)} %param.22) | copy-start | bytes 9437188
  0.0 3.3 %copy-start.14 = (s32[1,1,8]{2,1,0:T(1,128)S(1)}, s32[1,1,8]{2,1,0:T(1,128)}, u32[]{:S(2)}) copy-start(s32[1,1,8]{2,1,0:T(1,128)} %param.25) | copy-start | bytes 100
  1.0 7.1 %copy-start.10 = (s32[16]{0:T(128)}, s32[16]{0:T(128)S(1)}, u32[]{:S(2)}) copy-start(s32[16]{0:T(128)S(1)} %reshape_squeeze.3) | copy-start | bytes 196
  1.0 7.1 %copy-start.7 = (pred[16]{0:T(512)(128)(4,1)}, pred[16]{0:T(512)(128)(4,1)S(1)}, u32[]{:S(2)}) copy-start(pred[16]{0:T(512)(128)(4,1)S(1)} %compare_and_fusion.1) | copy-start | bytes 52
  3.3 17.5 %copy-start.5 = (s32[1,1,56,3]{2,1,3,0:T(1,128)S(1)}, s32[1,1,56,3]{2,1,3,0:T(1,128)}, u32[]{:S(2)}) copy-start(s32[1,1,56,3]{2,1,3,0:T(1,128)} %param.21) | copy-start | bytes 2020
  8.1 21.8 %all-to-all-start = ((bf16[8,2,128,128]{2,3,1,0:T(8,128)(2,1)}), bf16[8,2,128,128]{2,3,1,0:T(8,128)(2,1)}, u32[]{:S(2)}, u32[]{:S(2)}) async-start(bf16[8,2,128,128]{2,3,1,0:T(8,128)(2,1)} %bitcast.106), calls=%async_computation | async-start | bytes 1048576 | tf_op jit(solution)/shard_map/all_to_all | solution.py:27
  16.1 8.3 %collective-permute-start = (bf16[4,128,128]{1,2,0:T(8,128)(2,1)}, bf16[4,128,128]{1,2,0:T(8,128)(2,1)S(1)}, u32[]{:S(2)}, u32[]{:S(2)}) collective-permute-start(bf16[4,128,128]{1,2,0:T(8,128)(2,1)} %get-tuple-element.63), channel_id=1, source_target_pairs={{0,8},{8,16},{16,24},{1,9},{9,17},{17,25},{2,10},{10,18},{18,26},{... | collective-permute-start | bytes 393224 | tf_op jit(solution)/shard_map/ppermute | solution.py:17
  19.5 8.4 %collective-permute-start.1 = (bf16[4,128,128]{1,2,0:T(8,128)(2,1)S(1)}, bf16[4,128,128]{1,2,0:T(8,128)(2,1)S(1)}, u32[]{:S(2)}, u32[]{:S(2)}) collective-permute-start(bf16[4,128,128]{1,2,0:T(8,128)(2,1)S(1)} %get-tuple-element.64), channel_id=1, source_target_pairs={{8,0},{16,8},{24,16},{9,1},{17,9},{25,17},{10,2},{18,10},{26,18},{... | collective-permute-start | bytes 393224 | tf_op jit(solution)/shard_map/ppermute | solution.py:19
  32.8 9.3 %copy-start.3 = (pred[56,3]{1,0:T(8,128)(4,1)S(1)}, pred[56,3]{1,0:T(8,128)(4,1)}, u32[]{:S(2)}) copy-start(pred[56,3]{1,0:T(8,128)(4,1)} %copy.19) | copy-start | bytes 508
  48.7 1.2 copy-start.2
  52.9 20.4 %all-to-all-start.1 = ((bf16[8,2,128,128]{3,2,1,0:T(8,128)(2,1)}), bf16[8,2,128,128]{3,2,1,0:T(8,128)(2,1)}, u32[]{:S(2)}, u32[]{:S(2)}) async-start(bf16[8,2,128,128]{3,2,1,0:T(8,128)(2,1)} %copy.25), calls=%async_computation.1 | async-start | bytes 1048576 | tf_op jit(solution)/shard_map/all_to_all | solution.py:27
  58.0 15.3 %copy-start.11 = (s32[16]{0:T(128)S(1)}, s32[16]{0:T(128)}, u32[]{:S(2)}) copy-start(s32[16]{0:T(128)} %copy-done.10) | copy-start | bytes 196
  58.0 7.5 %collective-permute-start.2 = (bf16[4,128,128]{1,2,0:T(8,128)(2,1)S(1)}, bf16[4,128,128]{1,2,0:T(8,128)(2,1)S(1)}, u32[]{:S(2)}, u32[]{:S(2)}) collective-permute-start(bf16[4,128,128]{1,2,0:T(8,128)(2,1)S(1)} %get-tuple-element.58), channel_id=1, source_target_pairs={{0,8},{8,16},{16,24},{1,9},{9,17},{17,25},{2,10},{10,18},{18,26},{... | collective-permute-start | bytes 393224 | tf_op jit(solution)/shard_map/ppermute | solution.py:17
  64.2 7.4 %collective-permute-start.3 = (bf16[4,128,128]{1,2,0:T(8,128)(2,1)S(1)}, bf16[4,128,128]{1,2,0:T(8,128)(2,1)S(1)}, u32[]{:S(2)}, u32[]{:S(2)}) collective-permute-start(bf16[4,128,128]{1,2,0:T(8,128)(2,1)S(1)} %get-tuple-element.57), channel_id=1, source_target_pairs={{8,0},{16,8},{24,16},{9,1},{17,9},{25,17},{10,2},{18,10},{26,18},{... | collective-permute-start | bytes 393224 | tf_op jit(solution)/shard_map/ppermute | solution.py:19
  79.3 6.3 %copy-start.8 = (pred[16]{0:T(512)(128)(4,1)S(1)}, pred[16]{0:T(512)(128)(4,1)}, u32[]{:S(2)}) copy-start(pred[16]{0:T(512)(128)(4,1)} %copy-done.7) | copy-start | bytes 52
  82.9 9.4 %copy-start.6 = (s32[1,1,32,3]{2,1,3,0:T(1,128)S(1)}, s32[1,1,32,3]{2,1,3,0:T(1,128)}, u32[]{:S(2)}) copy-start(s32[1,1,32,3]{2,1,3,0:T(1,128)} %param.23) | copy-start | bytes 1156
  87.6 20.2 %all-to-all-start.2 = ((bf16[8,2,128,128]{2,3,1,0:T(8,128)(2,1)}), bf16[8,2,128,128]{2,3,1,0:T(8,128)(2,1)}, u32[]{:S(2)}, u32[]{:S(2)}) async-start(bf16[8,2,128,128]{2,3,1,0:T(8,128)(2,1)} %bitcast.107), calls=%async_computation.2 | async-start | bytes 1048576 | tf_op jit(solution)/shard_map/all_to_all | solution.py:27
  94.6 10.8 %collective-permute-start.4 = (bf16[4,128,128]{1,2,0:T(8,128)(2,1)}, bf16[4,128,128]{1,2,0:T(8,128)(2,1)S(1)}, u32[]{:S(2)}, u32[]{:S(2)}) collective-permute-start(bf16[4,128,128]{1,2,0:T(8,128)(2,1)} %get-tuple-element.61), channel_id=1, source_target_pairs={{0,8},{8,16},{16,24},{1,9},{9,17},{17,25},{2,10},{10,18},{18,26},{... | collective-permute-start | bytes 393224 | tf_op jit(solution)/shard_map/ppermute | solution.py:17
  98.8 7.5 %collective-permute-start.5 = (bf16[4,128,128]{1,2,0:T(8,128)(2,1)S(1)}, bf16[4,128,128]{1,2,0:T(8,128)(2,1)S(1)}, u32[]{:S(2)}, u32[]{:S(2)}) collective-permute-start(bf16[4,128,128]{1,2,0:T(8,128)(2,1)S(1)} %get-tuple-element.62), channel_id=1, source_target_pairs={{8,0},{16,8},{24,16},{9,1},{17,9},{25,17},{10,2},{18,10},{26,18},{... | collective-permute-start | bytes 393224 | tf_op jit(solution)/shard_map/ppermute | solution.py:19
  110.7 4.2 %copy-start.13 = (pred[32,3]{1,0:T(8,128)(4,1)S(1)}, pred[32,3]{1,0:T(8,128)(4,1)}, u32[]{:S(2)}) copy-start(pred[32,3]{1,0:T(8,128)(4,1)} %copy.29) | copy-start | bytes 292
  114.8 7.3 %copy-start.9 = (pred[16]{0:T(512)(128)(4,1)S(1)}, pred[16]{0:T(512)(128)(4,1)}, u32[]{:S(2)}) copy-start(pred[16]{0:T(512)(128)(4,1)} %copy-done.7) | copy-start | bytes 52
  124.1 19.5 %all-to-all-start.3 = ((bf16[8,2,128,128]{2,3,1,0:T(8,128)(2,1)}), bf16[8,2,128,128]{2,3,1,0:T(8,128)(2,1)}, u32[]{:S(2)}, u32[]{:S(2)}) async-start(bf16[8,2,128,128]{2,3,1,0:T(8,128)(2,1)} %bitcast.108), calls=%async_computation.3 | async-start | bytes 1048576 | tf_op jit(solution)/shard_map/all_to_all | solution.py:27
  129.2 7.6 %collective-permute-start.6 = (bf16[4,128,128]{1,2,0:T(8,128)(2,1)S(1)}, bf16[4,128,128]{1,2,0:T(8,128)(2,1)S(1)}, u32[]{:S(2)}, u32[]{:S(2)}) collective-permute-start(bf16[4,128,128]{1,2,0:T(8,128)(2,1)S(1)} %get-tuple-element.59), channel_id=1, source_target_pairs={{0,8},{8,16},{16,24},{1,9},{9,17},{17,25},{2,10},{10,18},{18,26},{... | collective-permute-start | bytes 393224 | tf_op jit(solution)/shard_map/ppermute | solution.py:17
  133.5 7.4 %collective-permute-start.7 = (bf16[4,128,128]{1,2,0:T(8,128)(2,1)S(1)}, bf16[4,128,128]{1,2,0:T(8,128)(2,1)S(1)}, u32[]{:S(2)}, u32[]{:S(2)}) collective-permute-start(bf16[4,128,128]{1,2,0:T(8,128)(2,1)S(1)} %get-tuple-element.60), channel_id=1, source_target_pairs={{8,0},{16,8},{24,16},{9,1},{17,9},{25,17},{10,2},{18,10},{26,18},{... | collective-permute-start | bytes 393224 | tf_op jit(solution)/shard_map/ppermute | solution.py:19
  146.4 9.3 %copy-start.4 = (pred[56,3]{1,0:T(8,128)(4,1)S(1)}, pred[56,3]{1,0:T(8,128)(4,1)}, u32[]{:S(2)}) copy-start(pred[56,3]{1,0:T(8,128)(4,1)} %copy.19) | copy-start | bytes 508
  162.4 1.2 copy-start.1
  166.5 21.3 %all-to-all-start.4 = ((bf16[8,2,128,128]{3,2,1,0:T(8,128)(2,1)}), bf16[8,2,128,128]{3,2,1,0:T(8,128)(2,1)}, u32[]{:S(2)}, u32[]{:S(2)}) async-start(bf16[8,2,128,128]{3,2,1,0:T(8,128)(2,1)} %copy.32), calls=%async_computation.4 | async-start | bytes 1048576 | tf_op jit(solution)/shard_map/all_to_all | solution.py:27
  171.6 16.2 %copy-start.12 = (s32[16]{0:T(128)S(1)}, s32[16]{0:T(128)}, u32[]{:S(2)}) copy-start(s32[16]{0:T(128)} %copy-done.10) | copy-start | bytes 196
  171.6 8.4 %collective-permute-start.8 = (bf16[4,128,128]{1,2,0:T(8,128)(2,1)S(1)}, bf16[4,128,128]{1,2,0:T(8,128)(2,1)S(1)}, u32[]{:S(2)}, u32[]{:S(2)}) collective-permute-start(bf16[4,128,128]{1,2,0:T(8,128)(2,1)S(1)} %get-tuple-element.56), channel_id=1, source_target_pairs={{0,8},{8,16},{16,24},{1,9},{9,17},{17,25},{2,10},{10,18},{18,26},{... | collective-permute-start | bytes 393224 | tf_op jit(solution)/shard_map/ppermute | solution.py:17
  178.8 7.4 %collective-permute-start.9 = (bf16[4,128,128]{1,2,0:T(8,128)(2,1)S(1)}, bf16[4,128,128]{1,2,0:T(8,128)(2,1)S(1)}, u32[]{:S(2)}, u32[]{:S(2)}) collective-permute-start(bf16[4,128,128]{1,2,0:T(8,128)(2,1)S(1)} %get-tuple-element.55), channel_id=1, source_target_pairs={{8,0},{16,8},{24,16},{9,1},{17,9},{25,17},{10,2},{18,10},{26,18},{... | collective-permute-start | bytes 393224 | tf_op jit(solution)/shard_map/ppermute | solution.py:19
where the time goes:
time: 202 us; the launch traced here: 200 us
  local copies, waits for them, and re-layouts  63.8 us (32%)
  starting transfers between devices  49.8 us (25%)
  other arithmetic  37.1 us (18%)
  waiting for transfers between devices  25.3 us (13%)
  matrix products  23.9 us (12%)
    all_to_all x5, starting transfers between devices, route(): lax.all_to_all(buffer, 'cross', split_axis=0, concat_axis=0, tiled=True)  23.5 us
    gather x3, local copies, waits for them, and re-layouts, apply_set(): picked = jnp.take(extended, columns, axis=0)  22.8 us
    ppermute x5, starting transfers between devices, extended_2(): lax.ppermute(tail, axis, [(i, (i + 1) % count) for i in range(ends)])  19.7 us
    dot_general x3, matrix products, apply_set(): lax.dot_general(blocks, picked, (((1, 3), (1, 2)), ((0,), (0,))), preferr...  17.9 us
    ppermute x5, waiting for transfers between devices, extended_2(): lax.ppermute(head, axis, [((i + 1) % count, i) for i in range(ends)])  17.4 us
    concatenate x3, other arithmetic, extend(): jnp.concatenate([field, padded[:OVL], padded[owned + OVL:], incoming.resh...  8.61 us
    gather x3, local copies, waits for them, and re-layouts, extend(): outgoing = jnp.take(field, flat_targets, axis=0)  7.97 us
    ppermute x5, starting transfers between devices, extended_2(): lax.ppermute(head, axis, [((i + 1) % count, i) for i in range(ends)])  6.62 us
  transfers between devices with their start and end apart: 15, of which 9 were waited for; matrix products, arithmetic and copies ran while one was open for 14% of the time, Pallas kernels for 0%

commit v1 on v0

v1 whole, which is shorter than its diff:
```python
import functools

import jax
import jax.numpy as jnp
from jax import lax
from jax.experimental import pallas as pl
from jax.experimental.pallas import tpu as pltpu
from jax.sharding import PartitionSpec as P

MESH = pl.DeviceIdType.MESH
F32 = jnp.float32
BF16 = jnp.bfloat16


def kernel(
    n_slab, n, ovl,
    rhs_hbm, m_hbm, j_hbm, m_cols, j_cols, targets, counts,
    out_ref,
    m_v, j_v, own0, own1, own2, ext0, ext1, ext2, part, send_buf, ret, ret_slab, run, acc,
    prev, last, load_sem, send_sem, recv_sem,
):
    s = lax.axis_index("slab")
    c = lax.axis_index("cross")
    own = (own0, own1, own2)
    ext = (ext0, ext1, ext2)
    rows = own0.shape[0]
    cap = send_buf.shape[2]
    kcount = m_v.shape[1]
    base = rows + 2 * ovl
    slots = (n - 1) * cap
    zero_slot = slots
    up_i, down_i = n, n + 1
    has_up = s > 0
    has_down = s < n_slab - 1

    def peer(d):
        return lax.rem(c + d, n)

    def order(t):
        return n // 2 + (1 - 2 * lax.rem(t, 2)) * ((t + 1) // 2)

    load_own = pltpu.make_async_copy(rhs_hbm.at[0, 0], own0, load_sem.at[0])
    load_ext = pltpu.make_async_copy(rhs_hbm.at[0, 0], ext0.at[pl.ds(0, rows)], load_sem.at[1])
    load_m = pltpu.make_async_copy(m_hbm.at[0, 0], m_v, load_sem.at[2])
    load_j = pltpu.make_async_copy(j_hbm.at[0, 0], j_v, load_sem.at[3])
    load_own.start()
    load_ext.start()
    load_m.start()
    load_j.start()

    barrier = pltpu.get_barrier_semaphore()

    @pl.loop(1, n)
    def _(d):
        pl.semaphore_signal(barrier, inc=1, device_id=(s, peer(d)), device_id_type=MESH)

    @pl.when(has_up)
    def _():
        pl.semaphore_signal(barrier, inc=1, device_id=(s - 1, c), device_id_type=MESH)

    @pl.when(has_down)
    def _():
        pl.semaphore_signal(barrier, inc=1, device_id=(s + 1, c), device_id_type=MESH)

    zero_tile = jnp.zeros(own0.shape[1:], BF16)
    for r in range(3):
        for t in range(cap):
            ext[r][base + c * cap + t] = zero_tile

    @pl.when(jnp.logical_not(has_up))
    def _():
        for r in range(3):
            for t in range(ovl):
                ext[r][rows + t] = zero_tile
        for r in range(2):
            for t in range(ovl):
                ret_slab[r, t] = zero_tile

    @pl.when(jnp.logical_not(has_down))
    def _():
        for r in range(3):
            for t in range(ovl):
                ext[r][rows + ovl + t] = zero_tile
        for r in range(2):
            for t in range(ovl):
                ret_slab[r, ovl + t] = zero_tile

    run[zero_slot] = jnp.zeros(own0.shape[1:], F32)

    def slab_copy(src, dst, r, mine, theirs, to):
        return pltpu.make_async_remote_copy(
            src_ref=src, dst_ref=dst, send_sem=send_sem.at[r, mine], recv_sem=recv_sem.at[r, theirs],
            device_id=(to, c), device_id_type=MESH,
        )

    def lend_up(e, r):
        return slab_copy(ext[e].at[pl.ds(0, ovl)], ext[e].at[pl.ds(rows + ovl, ovl)], r, up_i, down_i, s - 1)

    def lend_down(e, r):
        return slab_copy(ext[e].at[pl.ds(rows - ovl, ovl)], ext[e].at[pl.ds(rows, ovl)], r, down_i, up_i, s + 1)

    def lend_cross(e, r, d):
        return pltpu.make_async_remote_copy(
            src_ref=send_buf.at[e, d - 1], dst_ref=ext[e].at[pl.ds(base + c * cap, cap)],
            send_sem=send_sem.at[r, d], recv_sem=recv_sem.at[r, n - d],
            device_id=(s, peer(d)), device_id_type=MESH,
        )

    def got_cross(e, r, d):
        return pltpu.make_async_remote_copy(
            src_ref=send_buf.at[e, d - 1], dst_ref=ext[e].at[pl.ds(base + peer(d) * cap, cap)],
            send_sem=send_sem.at[r, d], recv_sem=recv_sem.at[r, d],
            device_id=(s, peer(d)), device_id_type=MESH,
        )

    def got_up(e, r):
        return slab_copy(ext[e].at[pl.ds(0, ovl)], ext[e].at[pl.ds(rows, ovl)], r, up_i, up_i, s - 1)

    def got_down(e, r):
        return slab_copy(ext[e].at[pl.ds(0, ovl)], ext[e].at[pl.ds(rows + ovl, ovl)], r, down_i, down_i, s + 1)

    def lend_slab(e, r):
        @pl.when(has_up)
        def _():
            lend_up(e, r).start()

        @pl.when(has_down)
        def _():
            lend_down(e, r).start()

    def lend_rows(e, r):
        @pl.loop(0, n - 1)
        def _(step):
            d = order(step)
            q = peer(d)
            for t in range(cap):
                picked = own[e][targets[0, 0, t, q]]
                used = t < counts[0, 0, q]
                send_buf[e, d - 1, t] = jnp.where(used, picked, jnp.zeros_like(picked))
            lend_cross(e, r, d).start()

    def await_lent(e, r):
        @pl.when(has_up)
        def _():
            got_up(e, r).wait_recv()

        @pl.when(has_down)
        def _():
            got_down(e, r).wait_recv()

        @pl.loop(1, n)
        def _(d):
            got_cross(e, r, d).wait_recv()

    def finish_lend(e, r):
        @pl.when(has_up)
        def _():
            lend_up(e, r).wait_send()

        @pl.when(has_down)
        def _():
            lend_down(e, r).wait_send()

        @pl.loop(1, n)
        def _(d):
            lend_cross(e, r, d).wait_send()

    def back_up(a, r):
        return slab_copy(part.at[a, pl.ds(rows, ovl)], ret_slab.at[a, pl.ds(ovl, ovl)], r, up_i, down_i, s - 1)

    def back_down(a, r):
        return slab_copy(part.at[a, pl.ds(rows + ovl, ovl)], ret_slab.at[a, pl.ds(0, ovl)], r, down_i, up_i, s + 1)

    def home_up(a, r):
        return slab_copy(part.at[a, pl.ds(rows, ovl)], ret_slab.at[a, pl.ds(0, ovl)], r, up_i, up_i, s - 1)

    def home_down(a, r):
        return slab_copy(part.at[a, pl.ds(rows, ovl)], ret_slab.at[a, pl.ds(ovl, ovl)], r, down_i, down_i, s + 1)

    def back_cross(a, r, d):
        return pltpu.make_async_remote_copy(
            src_ref=part.at[a, pl.ds(base + peer(d) * cap, cap)], dst_ref=ret.at[a, n - d - 1],
            send_sem=send_sem.at[r, d], recv_sem=recv_sem.at[r, n - d],
            device_id=(s, peer(d)), device_id_type=MESH,
        )

    def home_cross(a, r, d):
        return pltpu.make_async_remote_copy(
            src_ref=part.at[a, pl.ds(base + peer(d) * cap, cap)], dst_ref=ret.at[a, d - 1],
            send_sem=send_sem.at[r, d], recv_sem=recv_sem.at[r, d],
            device_id=(s, peer(d)), device_id_type=MESH,
        )

    def row_product(blocks, cols, e, i, k0=0):
        left = jnp.concatenate([blocks[i, k] for k in range(k0, kcount)], axis=1)
        right = jnp.concatenate([ext[e][cols[0, k, 0, i]] for k in range(k0, kcount)], axis=0)
        return jnp.dot(left, right, preferred_element_type=F32)

    def partial_row(a, e, i):
        part[a, i] = row_product(m_v, m_cols, e, i).astype(BF16)

    def apply_and_return(a, e, r):
        @pl.loop(0, n - 1)
        def _(step):
            d = order(step)
            first_row = base + peer(d) * cap
            for t in range(cap):
                partial_row(a, e, first_row + t)
            back_cross(a, r, d).start()

        @pl.loop(0, 2 * ovl // 4)
        def _(g):
            for t in range(4):
                partial_row(a, e, rows + 4 * g + t)

        @pl.when(has_up)
        def _():
            back_up(a, r).start()

        @pl.when(has_down)
        def _():
            back_down(a, r).start()

        @pl.loop(0, rows // 4)
        def _(g):
            for t in range(4):
                partial_row(a, e, 4 * g + t)

    def await_returns(a, r):
        @pl.loop(1, n)
        def _(d):
            home_cross(a, r, d).wait_recv()
            for t in range(cap):
                p = (d - 1) * cap + t
                run[p] = ret[a, d - 1, t].astype(F32) + run[prev[p]]

        @pl.when(has_up)
        def _():
            home_up(a, r).wait_recv()

        @pl.when(has_down)
        def _():
            home_down(a, r).wait_recv()

    def finish_return(a, r):
        @pl.when(has_up)
        def _():
            back_up(a, r).wait_send()

        @pl.when(has_down)
        def _():
            back_down(a, r).wait_send()

        @pl.loop(1, n)
        def _(d):
            back_cross(a, r, d).wait_send()

    def assembled(a, body):
        def total(i):
            return part[a, i].astype(F32) + run[last[i]]

        @pl.loop(0, ovl)
        def _(i):
            body(i, total(i) + ret_slab[a, i].astype(F32))

        @pl.loop(0, ovl)
        def _(t):
            i = rows - ovl + t
            body(i, total(i) + ret_slab[a, ovl + t].astype(F32))

        @pl.loop(ovl, rows - ovl)
        def _(i):
            body(i, total(i))

    load_own.wait()
    load_ext.wait()

    pl.semaphore_wait(barrier, n - 1 + has_up.astype(jnp.int32) + has_down.astype(jnp.int32))

    lend_slab(0, 0)
    lend_rows(0, 0)

    def key_of(p):
        q = peer(p // cap + 1)
        t = lax.rem(p, cap)
        return jnp.where(t < counts[0, 0, q], targets[0, 0, t, q], -1)

    @pl.loop(0, rows)
    def _(i):
        last[i] = zero_slot

    keys = [key_of(p) for p in range(slots)]
    for p in range(slots):
        found = zero_slot
        for p2 in range(p):
            found = jnp.where(keys[p2] == keys[p], p2, found)
        prev[p] = jnp.where(keys[p] < 0, zero_slot, found)

    @pl.loop(0, rows)
    def _(i):
        found = zero_slot
        for p in range(slots):
            found = jnp.where(keys[p] == i, p, found)
        last[i] = found

    load_m.wait()
    load_j.wait()
    await_lent(0, 0)

    apply_and_return(0, 0, 1)
    await_returns(0, 1)

    def put_first(i, value):
        rounded = value.astype(BF16)
        own[1][i] = rounded
        ext[1][i] = rounded

    assembled(0, put_first)

    lend_slab(1, 2)
    lend_rows(1, 2)

    @pl.loop(0, rows // 4)
    def _(g):
        for t in range(4):
            i = 4 * g + t
            acc[i] = own[0][i].astype(F32) - jnp.dot(j_v[i, 0], own[1][i], preferred_element_type=F32)

    await_lent(1, 2)

    @pl.loop(0, rows // 4)
    def _(g):
        for t in range(4):
            i = 4 * g + t
            rounded = (acc[i] - row_product(j_v, j_cols, 1, i, 1)).astype(BF16)
            own[2][i] = rounded
            ext[2][i] = rounded

    lend_slab(2, 3)
    lend_rows(2, 3)
    await_lent(2, 3)

    apply_and_return(1, 2, 4)
    await_returns(1, 4)

    def put_second(i, value):
        out_ref[0, 0, i] = (own[1][i].astype(F32) + value).astype(BF16)

    assembled(1, put_second)

    finish_lend(0, 0)
    finish_return(0, 1)
    finish_lend(1, 2)
    finish_lend(2, 3)
    finish_return(1, 4)


def solution(mesh):
    n_slab = mesh.shape["slab"]
    n = mesh.shape["cross"]

    def per_device(rhs, m_blocks, m_cols, j_blocks, j_cols, send_list, send_count):
        rows, blk, nv = rhs.shape[2:]
        total_rows, kcount = m_blocks.shape[2:4]
        cap = send_list.shape[3]
        ovl = (total_rows - rows - n * cap) // 2
        slots = (n - 1) * cap
        tile = (blk, nv)
        smem = pl.BlockSpec(memory_space=pltpu.SMEM)
        hbm = pl.BlockSpec(memory_space=pl.ANY)
        return pl.pallas_call(
            functools.partial(kernel, n_slab, n, ovl),
            out_shape=jax.ShapeDtypeStruct(rhs.shape, rhs.dtype),
            in_specs=[hbm, hbm, hbm, smem, smem, smem, smem],
            out_specs=pl.BlockSpec(memory_space=pltpu.VMEM),
            scratch_shapes=[
                pltpu.VMEM(m_blocks.shape[2:], BF16),
                pltpu.VMEM(j_blocks.shape[2:], BF16),
                *([pltpu.VMEM((rows,) + tile, BF16)] * 3),
                *([pltpu.VMEM((total_rows,) + tile, BF16)] * 3),
                pltpu.VMEM((2, total_rows) + tile, BF16),
                pltpu.VMEM((3, n - 1, cap) + tile, BF16),
                pltpu.VMEM((2, n - 1, cap) + tile, BF16),
                pltpu.VMEM((2, 2 * ovl) + tile, BF16),
                pltpu.VMEM((slots + 1,) + tile, F32),
                pltpu.VMEM((rows,) + tile, F32),
                pltpu.SMEM((slots,), jnp.int32),
                pltpu.SMEM((rows,), jnp.int32),
                pltpu.SemaphoreType.DMA((4,)),
                pltpu.SemaphoreType.DMA((5, n + 2)),
                pltpu.SemaphoreType.DMA((5, n + 2)),
            ],
            compiler_params=pltpu.CompilerParams(
                collective_id=0, has_side_effects=True, vmem_limit_bytes=60 * 1024 * 1024
            ),
        )(
            rhs, m_blocks, j_blocks, m_cols.transpose(0, 3, 1, 2), j_cols.transpose(0, 3, 1, 2),
            send_list.transpose(0, 1, 3, 2), send_count,
        )

    return jax.shard_map(
        per_device,
        mesh=mesh,
        in_specs=(
            P("slab", "cross", None, None, None),
            P("slab", "cross", None, None, None, None),
            P("slab", "cross", None, None),
            P("slab", "cross", None, None, None, None),
            P("slab", "cross", None, None),
            P("slab", "cross", None, None),
            P("slab", "cross", None),
        ),
        out_specs=P("slab", "cross", None, None, None),
        check_vma=False,
    )
```

time: 202 us -> 71.1 us (0.35)
  Pallas kernels: 0 us -> 67.9 us
  local copies, waits for them, and re-layouts: 63.8 us -> 2.31 us
  starting transfers between devices: 49.8 us -> 0 us
  other arithmetic: 37.1 us -> 0 us
  waiting for transfers between devices: 25.3 us -> 0 us
  matrix products: 23.9 us -> 0 us
    pallas_call x0 -> x1, Pallas kernels: none -> 67.9 us  [per_device(): pl.pallas_call(functools.partial(kernel, n_slab, n, ovl), out_shape=jax.S...]
    gather x6 -> x0, local copies, waits for them, and re-layouts: 30.8 us -> none  [the longest x3 22.8 us: apply_set(): picked = jnp.take(extended, columns, axis=0)]
    ppermute x10 -> x0, starting transfers between devices: 26.3 us -> none  [the longest x5 19.7 us: extended_2(): lax.ppermute(tail, axis, [(i, (i + 1) % count) for i in range(ends)])]
    dot_general x5 -> x0, matrix products: 23.9 us -> none  [the longest x3 17.9 us: apply_set(): lax.dot_general(blocks, picked, (((1, 3), (1, 2)), ((0,), (0,))), preferr...]
    all_to_all x5 -> x0, starting transfers between devices: 23.5 us -> none  [route(): lax.all_to_all(buffer, 'cross', split_axis=0, concat_axis=0, tiled=True)]
    ppermute x10 -> x0, waiting for transfers between devices: 19.2 us -> none  [the longest x5 17.4 us: extended_2(): lax.ppermute(head, axis, [((i + 1) % count, i) for i in range(ends)])]
    convert_element_type x3 -> x0, other arithmetic: 9.23 us -> none  [the longest x2 5.59 us: precondition(): total = partial_value[:owned].astype(jnp.float32)]
    concatenate x3 -> x0, other arithmetic: 8.61 us -> none  [extend(): jnp.concatenate([field, padded[:OVL], padded[owned + OVL:], incoming.resh...]
  transfers between devices with their start and end apart: 15 -> 0, of which waited for: 9 -> 0; matrix products, arithmetic and copies ran while one was open for 14% -> 0% of each run, Pallas kernels for 0% -> 0%
where the time goes in v1:
time: 71.1 us; the launch traced here: 70.2 us
  Pallas kernels  67.9 us (95%)
  local copies, waits for them, and re-layouts  2.31 us (3%)
    pallas_call x1, Pallas kernels, per_device(): pl.pallas_call(functools.partial(kernel, n_slab, n, ovl), out_shape=jax.S...  67.9 us
    unnamed x1, local copies, waits for them, and re-layouts  2.31 us

profile of v1, /device:TPU:0, one launch (start us, length us, event | category | flops | bytes accessed | tf_op | source)
XLA Modules:
  0.0 70.2 jit_solution(16114561713626224537)
XLA Ops:
  0.0 67.9 %shard_map.73 = bf16[1,1,32,128,128]{4,3,2,1,0:T(8,128)(2,1)} custom-call(bf16[1,1,32,128,128]{4,3,2,1,0:T(8,128)(2,1)} %rhs_hbm.1, bf16[1,1,56,3,128,128]{5,4,3,2,1,0:T(8,128)(2,1)} %m_hbm.1, bf16[1,1,32,3,128,128]{5,4,3,2,1,0:T(8,128)(2,1)} %j_hbm.1, s32[1,3,1,56]{3,2,1,0:T(1,128)} %bitcast.3, s32[1,3,1,32]{3,2,1,0:T(1,128)} %bitcast.4, ...), custom_call_target="tpu_custom_call" | custom-call | tf_op jit(solution)/shard_map/pallas_call | solution.py:371
  67.9 2.3 %copy.9 = bf16[1,1,32,128,128]{4,3,2,1,0:T(8,128)(2,1)} copy(bf16[1,1,32,128,128]{4,3,2,1,0:T(8,128)(2,1)} %shard_map.73) | data formatting | bytes 2097152

commit v2 on v1

v2 whole, which is shorter than its diff:
```python
import functools

import jax
import jax.numpy as jnp
from jax import lax
from jax.experimental import pallas as pl
from jax.experimental.pallas import tpu as pltpu
from jax.sharding import PartitionSpec as P

MESH = pl.DeviceIdType.MESH
F32 = jnp.float32
BF16 = jnp.bfloat16


def kernel(
    n_slab, n, ovl,
    rhs_hbm, m_hbm, j_hbm, m_cols, j_cols, targets, counts,
    out_ref,
    m_v, j_v, raw, own1a, own1b, own2a, own2b, ext0a, ext0b, ext1a, ext1b, ext2a, ext2b, part, send_buf, ret, ret_slab, run, acc,
    prev, last, load_sem, send_sem, recv_sem,
):
    s = lax.axis_index("slab")
    c = lax.axis_index("cross")
    own = ((raw, raw), (own1a, own1b), (own2a, own2b))
    ext = ((ext0a, ext0b), (ext1a, ext1b), (ext2a, ext2b))
    rows = raw.shape[0]
    halves = (0, 1)
    width = ext0a.shape[1]
    tile = ext0a.shape[1:]
    cap = send_buf.shape[3]
    kcount = m_v.shape[1]
    base = rows + 2 * ovl
    slots = (n - 1) * cap
    zero_slot = slots
    up_i, down_i = n, n + 1
    has_up = s > 0
    has_down = s < n_slab - 1

    def peer(d):
        return lax.rem(c + d, n)

    def order(t):
        return n // 2 + (1 - 2 * lax.rem(t, 2)) * ((t + 1) // 2)

    load_own = pltpu.make_async_copy(rhs_hbm.at[0, 0], raw, load_sem.at[0])
    load_m = pltpu.make_async_copy(m_hbm.at[0, 0], m_v, load_sem.at[1])
    load_j = pltpu.make_async_copy(j_hbm.at[0, 0], j_v, load_sem.at[2])
    load_own.start()
    load_m.start()
    load_j.start()

    barrier = pltpu.get_barrier_semaphore()

    @pl.loop(1, n)
    def _(d):
        pl.semaphore_signal(barrier, inc=1, device_id=(s, peer(d)), device_id_type=MESH)

    @pl.when(has_up)
    def _():
        pl.semaphore_signal(barrier, inc=1, device_id=(s - 1, c), device_id_type=MESH)

    @pl.when(has_down)
    def _():
        pl.semaphore_signal(barrier, inc=1, device_id=(s + 1, c), device_id_type=MESH)

    zero_tile = jnp.zeros(tile, BF16)
    for h in halves:
        for r in range(3):
            for t in range(cap):
                ext[r][h][base + c * cap + t] = zero_tile
        run[h, zero_slot] = jnp.zeros(tile, F32)

    def clear(start):
        for h in halves:
            for r in range(3):
                for t in range(ovl):
                    ext[r][h][rows + start + t] = zero_tile
            for r in range(2):
                for t in range(ovl):
                    ret_slab[r, h, start + t] = zero_tile

    @pl.when(jnp.logical_not(has_up))
    def _():
        clear(0)

    @pl.when(jnp.logical_not(has_down))
    def _():
        clear(ovl)

    def slab_copy(src, dst, r, h, mine, theirs, to):
        return pltpu.make_async_remote_copy(
            src_ref=src, dst_ref=dst, send_sem=send_sem.at[r, h, mine], recv_sem=recv_sem.at[r, h, theirs],
            device_id=(to, c), device_id_type=MESH,
        )

    def lend_up(e, r, h):
        return slab_copy(ext[e][h].at[pl.ds(0, ovl)], ext[e][h].at[pl.ds(rows + ovl, ovl)], r, h, up_i, down_i, s - 1)

    def lend_down(e, r, h):
        return slab_copy(ext[e][h].at[pl.ds(rows - ovl, ovl)], ext[e][h].at[pl.ds(rows, ovl)], r, h, down_i, up_i, s + 1)

    def lend_cross(e, r, h, d):
        return pltpu.make_async_remote_copy(
            src_ref=send_buf.at[e, h, d - 1], dst_ref=ext[e][h].at[pl.ds(base + c * cap, cap)],
            send_sem=send_sem.at[r, h, d], recv_sem=recv_sem.at[r, h, n - d],
            device_id=(s, peer(d)), device_id_type=MESH,
        )

    def got_cross(e, r, h, d):
        return pltpu.make_async_remote_copy(
            src_ref=send_buf.at[e, h, d - 1], dst_ref=ext[e][h].at[pl.ds(base + peer(d) * cap, cap)],
            send_sem=send_sem.at[r, h, d], recv_sem=recv_sem.at[r, h, d],
            device_id=(s, peer(d)), device_id_type=MESH,
        )

    def got_up(e, r, h):
        return slab_copy(ext[e][h].at[pl.ds(0, ovl)], ext[e][h].at[pl.ds(rows, ovl)], r, h, up_i, up_i, s - 1)

    def got_down(e, r, h):
        return slab_copy(ext[e][h].at[pl.ds(0, ovl)], ext[e][h].at[pl.ds(rows + ovl, ovl)], r, h, down_i, down_i, s + 1)

    def lend_slab(e, r, h):
        @pl.when(has_up)
        def _():
            lend_up(e, r, h).start()

        @pl.when(has_down)
        def _():
            lend_down(e, r, h).start()

    def lend_rows(e, r, h):
        @pl.loop(0, n - 1)
        def _(step):
            d = order(step)
            q = peer(d)
            for t in range(cap):
                picked = own[e][h][targets[0, 0, t, q]]
                used = t < counts[0, 0, q]
                send_buf[e, h, d - 1, t] = jnp.where(used, picked, jnp.zeros_like(picked))
            lend_cross(e, r, h, d).start()

    def await_lent(e, r, h):
        @pl.when(has_up)
        def _():
            got_up(e, r, h).wait_recv()

        @pl.when(has_down)
        def _():
            got_down(e, r, h).wait_recv()

        @pl.loop(1, n)
        def _(d):
            got_cross(e, r, h, d).wait_recv()

    def finish_lend(e, r, h):
        @pl.when(has_up)
        def _():
            lend_up(e, r, h).wait_send()

        @pl.when(has_down)
        def _():
            lend_down(e, r, h).wait_send()

        @pl.loop(1, n)
        def _(d):
            lend_cross(e, r, h, d).wait_send()

    def back_up(a, r, h):
        return slab_copy(part.at[a, h, pl.ds(rows, ovl)], ret_slab.at[a, h, pl.ds(ovl, ovl)], r, h, up_i, down_i, s - 1)

    def back_down(a, r, h):
        return slab_copy(part.at[a, h, pl.ds(rows + ovl, ovl)], ret_slab.at[a, h, pl.ds(0, ovl)], r, h, down_i, up_i, s + 1)

    def home_up(a, r, h):
        return slab_copy(part.at[a, h, pl.ds(rows, ovl)], ret_slab.at[a, h, pl.ds(0, ovl)], r, h, up_i, up_i, s - 1)

    def home_down(a, r, h):
        return slab_copy(part.at[a, h, pl.ds(rows, ovl)], ret_slab.at[a, h, pl.ds(ovl, ovl)], r, h, down_i, down_i, s + 1)

    def back_cross(a, r, h, d):
        return pltpu.make_async_remote_copy(
            src_ref=part.at[a, h, pl.ds(base + peer(d) * cap, cap)], dst_ref=ret.at[a, h, n - d - 1],
            send_sem=send_sem.at[r, h, d], recv_sem=recv_sem.at[r, h, n - d],
            device_id=(s, peer(d)), device_id_type=MESH,
        )

    def home_cross(a, r, h, d):
        return pltpu.make_async_remote_copy(
            src_ref=part.at[a, h, pl.ds(base + peer(d) * cap, cap)], dst_ref=ret.at[a, h, d - 1],
            send_sem=send_sem.at[r, h, d], recv_sem=recv_sem.at[r, h, d],
            device_id=(s, peer(d)), device_id_type=MESH,
        )

    def row_product(blocks, cols, e, h, i, k0=0):
        left = jnp.concatenate([ext[e][h][cols[0, k, 0, i]] for k in range(k0, kcount)], axis=1)
        right = jnp.concatenate([blocks[i, k] for k in range(k0, kcount)], axis=1)
        return lax.dot_general(left, right, (((1,), (1,)), ((), ())), preferred_element_type=F32)

    def partial_row(a, e, h, i):
        part[a, h, i] = row_product(m_v, m_cols, e, h, i).astype(BF16)

    def apply_margins(a, e, r, h):
        @pl.loop(0, n - 1)
        def _(step):
            d = order(step)
            first_row = base + peer(d) * cap
            for t in range(cap):
                partial_row(a, e, h, first_row + t)
            back_cross(a, r, h, d).start()

        @pl.loop(0, 2 * ovl // 4)
        def _(g):
            for t in range(4):
                partial_row(a, e, h, rows + 4 * g + t)

        @pl.when(has_up)
        def _():
            back_up(a, r, h).start()

        @pl.when(has_down)
        def _():
            back_down(a, r, h).start()

    def apply_owned(a, e, h):
        @pl.loop(0, rows // 4)
        def _(g):
            for t in range(4):
                partial_row(a, e, h, 4 * g + t)

    def await_returns(a, r, h):
        @pl.loop(1, n)
        def _(d):
            home_cross(a, r, h, d).wait_recv()
            for t in range(cap):
                p = (d - 1) * cap + t
                run[h, p] = ret[a, h, d - 1, t].astype(F32) + run[h, prev[p]]

        @pl.when(has_up)
        def _():
            home_up(a, r, h).wait_recv()

        @pl.when(has_down)
        def _():
            home_down(a, r, h).wait_recv()

    def finish_return(a, r, h):
        @pl.when(has_up)
        def _():
            back_up(a, r, h).wait_send()

        @pl.when(has_down)
        def _():
            back_down(a, r, h).wait_send()

        @pl.loop(1, n)
        def _(d):
            back_cross(a, r, h, d).wait_send()

    def assembled(a, h, body):
        def total(i):
            return part[a, h, i].astype(F32) + run[h, last[i]]

        @pl.loop(0, ovl)
        def _(i):
            body(h, i, total(i) + ret_slab[a, h, i].astype(F32))

        @pl.loop(0, ovl)
        def _(t):
            i = rows - ovl + t
            body(h, i, total(i) + ret_slab[a, h, ovl + t].astype(F32))

        @pl.loop(ovl, rows - ovl)
        def _(i):
            body(h, i, total(i))

    load_own.wait()

    def turn(i):
        turned = raw[i].T
        for h in halves:
            ext[0][h][i] = turned[h * width : (h + 1) * width]

    @pl.loop(0, ovl)
    def _(i):
        turn(i)
        turn(rows - ovl + i)

    pl.semaphore_wait(barrier, n - 1 + has_up.astype(jnp.int32) + has_down.astype(jnp.int32))

    for h in halves:
        lend_slab(0, 0, h)

    @pl.loop(0, n - 1)
    def _(step):
        d = order(step)
        q = peer(d)
        for t in range(cap):
            picked = raw[targets[0, 0, t, q]]
            used = t < counts[0, 0, q]
            turned = jnp.where(used, picked, jnp.zeros_like(picked)).T
            for h in halves:
                send_buf[0, h, d - 1, t] = turned[h * width : (h + 1) * width]
        lend_cross(0, 0, 0, d).start()

    @pl.loop(0, n - 1)
    def _(step):
        lend_cross(0, 0, 1, order(step)).start()

    @pl.loop(ovl, rows - ovl)
    def _(i):
        turn(i)

    def key_of(p):
        q = peer(p // cap + 1)
        t = lax.rem(p, cap)
        return jnp.where(t < counts[0, 0, q], targets[0, 0, t, q], -1)

    @pl.loop(0, rows)
    def _(i):
        last[i] = zero_slot

    keys = [key_of(p) for p in range(slots)]
    for p in range(slots):
        found = zero_slot
        for p2 in range(p):
            found = jnp.where(keys[p2] == keys[p], p2, found)
        prev[p] = jnp.where(keys[p] < 0, zero_slot, found)

    @pl.loop(0, rows)
    def _(i):
        found = zero_slot
        for p in range(slots):
            found = jnp.where(keys[p] == i, p, found)
        last[i] = found

    load_m.wait()
    load_j.wait()

    def put_first(h, i, value):
        rounded = value.astype(BF16)
        own[1][h][i] = rounded
        ext[1][h][i] = rounded

    def put_second(h, i, value):
        second = (own[1][h][i].astype(F32) + value).astype(BF16)
        out_ref[0, 0, i, :, h * width : (h + 1) * width] = second.T

    def first_and_lend(h):
        await_returns(0, 1, h)
        assembled(0, h, put_first)
        lend_slab(1, 2, h)
        lend_rows(1, 2, h)

    def residual_and_lend(h):
        @pl.loop(0, rows // 4)
        def _(g):
            for t in range(4):
                i = 4 * g + t
                image = lax.dot_general(
                    own[1][h][i], j_v[i, 0], (((1,), (1,)), ((), ())), preferred_element_type=F32
                )
                acc[i] = ext[0][h][i].astype(F32) - image

        await_lent(1, 2, h)

        @pl.loop(0, rows // 4)
        def _(g):
            for t in range(4):
                i = 4 * g + t
                rounded = (acc[i] - row_product(j_v, j_cols, 1, h, i, 1)).astype(BF16)
                own[2][h][i] = rounded
                ext[2][h][i] = rounded

        lend_slab(2, 3, h)
        lend_rows(2, 3, h)

    def second_half(h):
        await_returns(1, 4, h)
        assembled(1, h, put_second)

    for a, e, r, finish in ((0, 0, 0, first_and_lend), (1, 2, 3, second_half)):
        await_lent(e, r, 0)
        apply_margins(a, e, r + 1, 0)
        apply_owned(a, e, 0)
        await_lent(e, r, 1)
        apply_margins(a, e, r + 1, 1)
        if a == 1:
            apply_owned(a, e, 1)
        finish(0)
        if a == 0:
            apply_owned(a, e, 1)
        finish(1)
        if a == 0:
            residual_and_lend(0)
            residual_and_lend(1)

    for h in halves:
        finish_lend(0, 0, h)
        finish_return(0, 1, h)
        finish_lend(1, 2, h)
        finish_lend(2, 3, h)
        finish_return(1, 4, h)


def solution(mesh):
    n_slab = mesh.shape["slab"]
    n = mesh.shape["cross"]

    def per_device(rhs, m_blocks, m_cols, j_blocks, j_cols, send_list, send_count):
        rows, blk, nv = rhs.shape[2:]
        total_rows, kcount = m_blocks.shape[2:4]
        cap = send_list.shape[3]
        ovl = (total_rows - rows - n * cap) // 2
        slots = (n - 1) * cap
        tile = (nv // 2, blk)
        smem = pl.BlockSpec(memory_space=pltpu.SMEM)
        hbm = pl.BlockSpec(memory_space=pl.ANY)
        return pl.pallas_call(
            functools.partial(kernel, n_slab, n, ovl),
            out_shape=jax.ShapeDtypeStruct(rhs.shape, rhs.dtype),
            in_specs=[hbm, hbm, hbm, smem, smem, smem, smem],
            out_specs=pl.BlockSpec(memory_space=pltpu.VMEM),
            scratch_shapes=[
                pltpu.VMEM(m_blocks.shape[2:], BF16),
                pltpu.VMEM(j_blocks.shape[2:], BF16),
                pltpu.VMEM((rows, blk, nv), BF16),
                *([pltpu.VMEM((rows,) + tile, BF16)] * 4),
                *([pltpu.VMEM((total_rows,) + tile, BF16)] * 6),
                pltpu.VMEM((2, 2, total_rows) + tile, BF16),
                pltpu.VMEM((3, 2, n - 1, cap) + tile, BF16),
                pltpu.VMEM((2, 2, n - 1, cap) + tile, BF16),
                pltpu.VMEM((2, 2, 2 * ovl) + tile, BF16),
                pltpu.VMEM((2, slots + 1) + tile, F32),
                pltpu.VMEM((rows,) + tile, F32),
                pltpu.SMEM((slots,), jnp.int32),
                pltpu.SMEM((rows,), jnp.int32),
                pltpu.SemaphoreType.DMA((3,)),
                pltpu.SemaphoreType.DMA((5, 2, n + 2)),
                pltpu.SemaphoreType.DMA((5, 2, n + 2)),
            ],
            compiler_params=pltpu.CompilerParams(
                collective_id=0, has_side_effects=True, vmem_limit_bytes=60 * 1024 * 1024
            ),
        )(
            rhs, m_blocks, j_blocks, m_cols.transpose(0, 3, 1, 2), j_cols.transpose(0, 3, 1, 2),
            send_list.transpose(0, 1, 3, 2), send_count,
        )

    return jax.shard_map(
        per_device,
        mesh=mesh,
        in_specs=(
            P("slab", "cross", None, None, None),
            P("slab", "cross", None, None, None, None),
            P("slab", "cross", None, None),
            P("slab", "cross", None, None, None, None),
            P("slab", "cross", None, None),
            P("slab", "cross", None, None),
            P("slab", "cross", None),
        ),
        out_specs=P("slab", "cross", None, None, None),
        check_vma=False,
    )
```

time: 71.1 us -> 73.7 us (1.037); the launches traced: 70.2 us -> 73.5 us
  Pallas kernels: 67.9 us -> 71.2 us
    pallas_call x1, Pallas kernels: 67.9 us -> 71.2 us  [per_device(): pl.pallas_call(functools.partial(kernel, n_slab, n, ovl), out_shape=jax.S...]
where the time goes in v2:
time: 73.7 us; the launch traced here: 73.5 us
  Pallas kernels  71.2 us (97%)
  local copies, waits for them, and re-layouts  2.31 us (3%)
    pallas_call x1, Pallas kernels, per_device(): pl.pallas_call(functools.partial(kernel, n_slab, n, ovl), out_shape=jax.S...  71.2 us
    unnamed x1, local copies, waits for them, and re-layouts  2.31 us

profile of v2, /device:TPU:0, one launch (start us, length us, event | category | flops | bytes accessed | tf_op | source)
XLA Modules:
  0.0 73.5 jit_solution(14873983211372966075)
XLA Ops:
  0.0 71.2 %shard_map.73 = bf16[1,1,32,128,128]{4,3,2,1,0:T(8,128)(2,1)} custom-call(bf16[1,1,32,128,128]{4,3,2,1,0:T(8,128)(2,1)} %rhs_hbm.1, bf16[1,1,56,3,128,128]{5,4,3,2,1,0:T(8,128)(2,1)} %m_hbm.1, bf16[1,1,32,3,128,128]{5,4,3,2,1,0:T(8,128)(2,1)} %j_hbm.1, s32[1,3,1,56]{3,2,1,0:T(1,128)} %bitcast.3, s32[1,3,1,32]{3,2,1,0:T(1,128)} %bitcast.4, ...), custom_call_target="tpu_custom_call" | custom-call | tf_op jit(solution)/shard_map/pallas_call | solution.py:418
  71.2 2.3 %copy.9 = bf16[1,1,32,128,128]{4,3,2,1,0:T(8,128)(2,1)} copy(bf16[1,1,32,128,128]{4,3,2,1,0:T(8,128)(2,1)} %shard_map.73) | data formatting | bytes 2097152

commit v3 on v1

--- a/solution.py
+++ b/solution.py
@@ -260,17 +260,16 @@
             return part[a, i].astype(F32) + run[last[i]]
 
         @pl.loop(0, ovl)
-        def _(i):
-            body(i, total(i) + ret_slab[a, i].astype(F32))
-
-        @pl.loop(0, ovl)
         def _(t):
             i = rows - ovl + t
+            body(t, total(t) + ret_slab[a, t].astype(F32))
             body(i, total(i) + ret_slab[a, ovl + t].astype(F32))
 
-        @pl.loop(ovl, rows - ovl)
-        def _(i):
-            body(i, total(i))
+        @pl.loop(0, (rows - 2 * ovl) // 4)
+        def _(g):
+            for t in range(4):
+                i = ovl + 4 * g + t
+                body(i, total(i))
 
     load_own.wait()
     load_ext.wait()
@@ -367,10 +366,10 @@
         slots = (n - 1) * cap
         tile = (blk, nv)
         smem = pl.BlockSpec(memory_space=pltpu.SMEM)
-        hbm = pl.BlockSpec(memory_space=pl.ANY)
+        hbm = pl.BlockSpec(memory_space=pltpu.HBM)
         return pl.pallas_call(
             functools.partial(kernel, n_slab, n, ovl),
-            out_shape=jax.ShapeDtypeStruct(rhs.shape, rhs.dtype),
+            out_shape=pltpu.VMEM(rhs.shape, rhs.dtype),
             in_specs=[hbm, hbm, hbm, smem, smem, smem, smem],
             out_specs=pl.BlockSpec(memory_space=pltpu.VMEM),
             scratch_shapes=[

time: 71.1 us -> 68.5 us (0.963)
  local copies, waits for them, and re-layouts: 2.31 us -> 0.97 us
  Pallas kernels: 67.9 us -> 66.6 us
    unnamed x1, local copies, waits for them, and re-layouts: 2.31 us -> 0.97 us
    pallas_call x1, Pallas kernels: 67.9 us -> 66.6 us  [per_device(): pl.pallas_call(functools.partial(kernel, n_slab, n, ovl), out_shape=pltpu...]
where the time goes in v3:
time: 68.5 us; the launch traced here: 67.6 us
  Pallas kernels  66.6 us (97%)
  local copies, waits for them, and re-layouts  0.97 us (1%)
    pallas_call x1, Pallas kernels, per_device(): pl.pallas_call(functools.partial(kernel, n_slab, n, ovl), out_shape=pltpu...  66.6 us

profile of v3, /device:TPU:0, one launch (start us, length us, event | category | flops | bytes accessed | tf_op | source)
XLA Modules:
  0.0 67.6 jit_solution(3953023258326947498)
XLA Ops:
  0.0 66.6 %shard_map.73 = bf16[1,1,32,128,128]{4,3,2,1,0:T(8,128)(2,1)S(1)} custom-call(bf16[1,1,32,128,128]{4,3,2,1,0:T(8,128)(2,1)} %rhs_hbm.1, bf16[1,1,56,3,128,128]{5,4,3,2,1,0:T(8,128)(2,1)} %m_hbm.1, bf16[1,1,32,3,128,128]{5,4,3,2,1,0:T(8,128)(2,1)} %j_hbm.1, s32[1,3,1,56]{3,2,1,0:T(1,128)} %bitcast.3, s32[1,3,1,32]{3,2,1,0:T(1,128)} %bitcast.4, ...), custom_call_target="tpu_custom_call" | custom-call | tf_op jit(solution)/shard_map/pallas_call | solution.py:370
  66.6 1.0 %copy.9 = bf16[1,1,32,128,128]{4,3,2,1,0:T(8,128)(2,1)} copy(bf16[1,1,32,128,128]{4,3,2,1,0:T(8,128)(2,1)S(1)} %shard_map.73) | data formatting | bytes 2097152
